TPU v7x, 32 devices: a whole 2x2x4 slice. The times are simulated.
32 devices in a mesh: section: 4 (over y, core), ep: 8 (over z, x).
Axes of the slice: x: 2, y: 2, z: 4, core: 2. Of those that a mesh axis runs over, the one named last changes fastest.
Arguments:
- rows_in: bfloat16 [4, 64, 7168], P(None, 'ep'), may hold values from -6 to 6
- routes: int32 [4, 4, 64, 2], P('section', None, 'ep'), may hold values from 0 to 3, all different within a row; in each aligned block of 8 rows (0 to 7, 8 to 15, ..., all dimensions but the last counted through in order) at most 4 rows name the same one
- hot_blocks: int32 [4], P('section'), may hold values from 0 to 15
- gains: float32 [4, 7168], P('section'), may hold values from 0.1 to 1.9
- router: bfloat16 [4, 7168, 4], P('section'), may hold values from -0.0625 to 0.0625
- w_gate: bfloat16 [4, 7168, 4096], P('section', None, 'ep'), may hold values from -0.0625 to 0.0625
- w_up: bfloat16 [4, 7168, 4096], P('section', None, 'ep'), may hold values from -0.0625 to 0.0625
- w_down: bfloat16 [4, 4096, 7168], P('section', 'ep'), may hold values from -0.1875 to 0.1875
Outputs:
- section_rows: bfloat16 [4, 4, 64, 7168], P('section', None, 'ep')
- relative_load: float32 [4, 8], P('section', 'ep')
Inputs may be any that keep to these rules, and one draw needn't show every extreme that they name: `routes`: in every layer and micro-batch the 8 rows of one device name each expert at most 4 times.
All inputs are finite; a program needn't handle non-finite values.
Results may differ from a plain program's by a relative error of at most 0.025.
Values may be sent and summed in bfloat16 or wider, within the bound.
A program may use at most 128 MiB of HBM per device.

v0:
```python
import jax
import jax.numpy as jnp
from jax import lax
from jax.sharding import PartitionSpec as P

FFW = 1024
BLK = 256


def spread(block, axis, source):
    block = jnp.where(lax.axis_index(axis) == source, block, jnp.zeros_like(block))
    return lax.psum(block, axis)


def shifted(block, axis, distance):
    devices = range(lax.axis_size(axis))
    route = [(i - distance, i) for i in devices if i - distance in devices]
    return lax.ppermute(block, axis, route)


def local(rows_in, routes, hot_blocks, gains, router, w_gate, w_up, w_down):
    section_index = lax.axis_index("section")
    ep_index = lax.axis_index("ep")
    section_count = lax.axis_size("section")
    micro_count = rows_in.shape[0]
    tok_rows = rows_in.shape[1]
    model_width = rows_in.shape[2]
    columns = w_gate.shape[2]
    expert_count = router.shape[2]
    top_count = routes.shape[3]
    capacity = tok_rows // 2
    blocks_per_expert = FFW // BLK
    hot_index = hot_blocks[0]
    owner_index = hot_index // 2
    hot_expert = hot_index // blocks_per_expert
    norm_gain = gains[0]
    router_w = router[0]
    gate_w = w_gate[0]
    up_w = w_up[0]
    down_w = w_down[0]
    column_block = 2 * ep_index + lax.iota(jnp.int32, columns) // BLK
    keep_column = (column_block != hot_index)[None, :]
    expert_ids = lax.iota(jnp.int32, expert_count)
    block_start = hot_index % 2 * BLK
    copy_gate, copy_up, copy_down = (
        spread(lax.dynamic_slice_in_dim(gate_w, block_start, BLK, 1), "ep", owner_index),
        spread(lax.dynamic_slice_in_dim(up_w, block_start, BLK, 1), "ep", owner_index),
        spread(lax.dynamic_slice_in_dim(down_w, block_start, BLK, 0), "ep", owner_index),
    )

    def expert_rows(flat_rows):
        gate_value = jnp.dot(flat_rows, gate_w, preferred_element_type=jnp.float32)
        up_value = jnp.dot(flat_rows, up_w, preferred_element_type=jnp.float32)
        activation = (jax.nn.silu(gate_value) * up_value).astype(jnp.bfloat16)
        home_act = jnp.where(keep_column, activation, jnp.zeros_like(activation))
        return jnp.dot(home_act, down_w, preferred_element_type=jnp.float32).astype(jnp.bfloat16)

    def work_both(recv_parts):
        recv_rows, recv_flags = recv_parts
        sources = recv_rows.shape[0]
        item_count = recv_rows.shape[1]
        home_part = expert_rows(recv_rows.reshape(sources * item_count, model_width))
        home_part = home_part.reshape(sources, item_count, model_width)
        returned = lax.all_to_all(home_part, "ep", split_axis=0, concat_axis=0, tiled=True)
        filled = jnp.sum(recv_flags.astype(jnp.float32), axis=0, keepdims=True)
        return (returned, filled)

    def apply_layer(layer_input, route_ids):
        rows_float = layer_input.astype(jnp.float32)
        mean_square = jnp.mean(rows_float * rows_float, axis=-1, keepdims=True)
        normed = (rows_float * lax.rsqrt(mean_square + 1e-06) * norm_gain).astype(jnp.bfloat16)
        scores = jax.nn.sigmoid(jnp.dot(normed, router_w, preferred_element_type=jnp.float32))
        member = (route_ids[:, :, None] == expert_ids[None, None, :]).astype(jnp.float32)
        chosen = jnp.sum(member * scores[:, None, :], axis=2)
        gate_weights = 2.5 * chosen / jnp.sum(chosen, axis=1, keepdims=True)
        token_gate = jnp.sum(member * gate_weights[:, :, None], axis=1)
        routed = jnp.sum(member, axis=1)
        slot_rank = jnp.cumsum(routed, axis=0) - routed
        slot_ids = lax.iota(jnp.float32, capacity)
        placement = routed.T[:, None, :] * (
            slot_rank.T[:, None, :] == slot_ids[None, :, None]
        ).astype(jnp.float32)
        packed = jnp.einsum(
            "ect,tf->ecf",
            placement.astype(jnp.bfloat16),
            normed,
            preferred_element_type=jnp.float32,
        ).astype(jnp.bfloat16)
        slot_flags = jnp.sum(placement, axis=2).astype(jnp.bfloat16)
        send_rows = jnp.repeat(packed, 2, axis=0)
        send_flags = jnp.repeat(slot_flags, 2, axis=0)
        home_back, filled = work_both(
            (
                lax.all_to_all(send_rows, "ep", split_axis=0, concat_axis=0, tiled=True),
                lax.all_to_all(send_flags, "ep", split_axis=0, concat_axis=0, tiled=True),
            )
        )
        combined = home_back.astype(jnp.float32).reshape(expert_count, 2, capacity, model_width)
        pair_sum = combined[:, 0] + combined[:, 1]
        weighting = placement * token_gate.T[:, None, :]
        routed_sum = jnp.einsum("ect,ecf->tf", weighting, pair_sum, precision=lax.Precision.HIGHEST)
        local_gate = jnp.dot(normed, copy_gate, preferred_element_type=jnp.float32)
        local_up = jnp.dot(normed, copy_up, preferred_element_type=jnp.float32)
        local_act = (jax.nn.silu(local_gate) * local_up).astype(jnp.bfloat16)
        local_part = (
            jnp.dot(local_act, copy_down, preferred_element_type=jnp.float32)
            .astype(jnp.bfloat16)
            .astype(jnp.float32)
        )
        hot_gate = jnp.sum(jnp.where((expert_ids == hot_expert)[None, :], token_gate, 0.0), axis=1)
        routed_sum = routed_sum + hot_gate[:, None] * local_part
        own_hot = jnp.sum(jnp.where((expert_ids == hot_expert)[None, :], routed, 0.0))
        return ((rows_float + routed_sum).astype(jnp.bfloat16), jnp.sum(filled), own_hot)

    def run_tick(tick_index, loop_state):
        incoming, outputs, home_total, hot_total = loop_state
        micro_index = tick_index - section_index
        is_live = (micro_index >= 0) & (micro_index < micro_count)
        clipped = jnp.clip(micro_index, 0, micro_count - 1)
        fresh_rows = lax.dynamic_index_in_dim(rows_in, clipped, 0, keepdims=False)
        layer_input = jnp.where(section_index == 0, fresh_rows, incoming)
        route_ids = lax.dynamic_index_in_dim(routes[0], clipped, 0, keepdims=False)
        next_rows, home_rows, hot_rows = apply_layer(layer_input, route_ids)
        updated = lax.dynamic_update_index_in_dim(outputs, next_rows, clipped, 0)
        outputs = jnp.where(is_live, updated, outputs)
        home_total = home_total + jnp.where(is_live, home_rows, 0.0)
        hot_total = hot_total + jnp.where(is_live, hot_rows, 0.0)
        incoming = shifted(next_rows, "section", 1)
        return (incoming, outputs, home_total, hot_total)

    tick_count = micro_count + section_count - 1
    start_state = (
        jnp.zeros((tok_rows, model_width), jnp.bfloat16),
        jnp.zeros(rows_in.shape, jnp.bfloat16),
        jnp.float32(0.0),
        jnp.float32(0.0),
    )
    final_state = lax.fori_loop(0, tick_count, run_tick, start_state)
    outputs = final_state[1]
    unit_count = (
        final_state[2] * (2.0 - (owner_index == ep_index).astype(jnp.float32)) + final_state[3]
    )
    relative = unit_count / float(micro_count * tok_rows * top_count * blocks_per_expert)
    return (outputs[None], relative.reshape(1, 1))


def solution(mesh):
    return jax.shard_map(
        local,
        mesh=mesh,
        in_specs=(
            P(None, "ep", None),
            P("section", None, "ep", None),
            P("section"),
            P("section", None),
            P("section", None, None),
            P("section", None, "ep"),
            P("section", None, "ep"),
            P("section", "ep", None),
        ),
        out_specs=(P("section", None, "ep", None), P("section", "ep")),
        check_vma=False,
    )
```

profile of v0, /device:TPU:0, one launch (start us, length us, event | category | flops | bytes accessed | tf_op | source)
XLA Modules:
  0.0 818.4 jit_solution(853677512756800073)
XLA Ops:
  12.7 6.4 select_bitcast_fusion.1
  19.2 343.5 %all-reduce.3.cloned.1.call-done = (bf16[7168,256]{1,0:T(8,128)(2,1)}, bf16[7168,256]{1,0:T(8,128)(2,1)}, bf16[256,7168]{1,0:T(8,128)(2,1)}) async-done(((bf16[7168,256]{1,0:T(8,128)(2,1)}, bf16[7168,256]{1,0:T(8,128)(2,1)}, bf16[256,7168]{1,0:T(8,128)(2,1)}), (bf16[7168,256]{1,0:T(8,128)(2,1)}, bf16[7168,256]{1,0:T(8,128)(2,1)}, bf16[256,7168]{1,0:T(8,128)(2,1)})) %all-reduce.3.cloned.1.call-update) | async-done | bytes 11010064 | tf_op jit(solution)/shard_map/psum | solution.py:12
  362.8 446.8 %while.22 = (s32[]{:T(128)}, bf16[8,7168]{1,0:T(8,128)(2,1)S(1)}, bf16[4,8,7168]{2,1,0:T(8,128)(2,1)S(1)}, f32[]{:T(128)}, f32[]{:T(128)}, /*index=5*/pred[]{:T(...) while((s32[]{:T(128)}, bf16[8,7168]{1,0:T(8,128)(2,1)S(1)}, ...), condition=%wide.region_14.15_spmd.clone.clone, body=%wide.region_3.14_spmd.clone.clone.sunk | while | flops 808455232 | bytes 45640856 | solution.py:138
  371.2 11.8 %all-to-all-done = bf16[8,4,7168]{2,1,0:T(4,128)(2,1)S(1)} async-done(((bf16[8,4,7168]{2,1,0:T(4,128)(2,1)}), bf16[8,4,7168]{2,1,0:T(4,128)(2,1)S(1)}, u32[]{:S(2)}, u32[]{:S(2)}) %all-to-all-start) | async-done | bytes 458784 | tf_op jit(solution)/shard_map/while/body/eval_jaxpr/all_to_all | solution.py:94
  387.5 7.9 convolution_convert_fusion.6
  421.4 5.9 all-to-all-done.2
  436.8 12.2 %all-to-all-done = bf16[8,4,7168]{2,1,0:T(4,128)(2,1)S(1)} async-done(((bf16[8,4,7168]{2,1,0:T(4,128)(2,1)}), bf16[8,4,7168]{2,1,0:T(4,128)(2,1)S(1)}, u32[]{:S(2)}, u32[]{:S(2)}) %all-to-all-start) | async-done | bytes 458784 | tf_op jit(solution)/shard_map/while/body/eval_jaxpr/all_to_all | solution.py:94
  453.6 7.9 convolution_convert_fusion.6
  487.5 5.9 all-to-all-done.2
  502.9 10.7 %all-to-all-done = bf16[8,4,7168]{2,1,0:T(4,128)(2,1)S(1)} async-done(((bf16[8,4,7168]{2,1,0:T(4,128)(2,1)}), bf16[8,4,7168]{2,1,0:T(4,128)(2,1)S(1)}, u32[]{:S(2)}, u32[]{:S(2)}) %all-to-all-start) | async-done | bytes 458784 | tf_op jit(solution)/shard_map/while/body/eval_jaxpr/all_to_all | solution.py:94
  518.1 7.9 convolution_convert_fusion.6
  550.7 5.9 all-to-all-done.2
  566.1 10.5 %all-to-all-done = bf16[8,4,7168]{2,1,0:T(4,128)(2,1)S(1)} async-done(((bf16[8,4,7168]{2,1,0:T(4,128)(2,1)}), bf16[8,4,7168]{2,1,0:T(4,128)(2,1)S(1)}, u32[]{:S(2)}, u32[]{:S(2)}) %all-to-all-start) | async-done | bytes 458784 | tf_op jit(solution)/shard_map/while/body/eval_jaxpr/all_to_all | solution.py:94
  581.1 7.9 convolution_convert_fusion.6
  613.6 5.9 all-to-all-done.2
  629.1 10.5 %all-to-all-done = bf16[8,4,7168]{2,1,0:T(4,128)(2,1)S(1)} async-done(((bf16[8,4,7168]{2,1,0:T(4,128)(2,1)}), bf16[8,4,7168]{2,1,0:T(4,128)(2,1)S(1)}, u32[]{:S(2)}, u32[]{:S(2)}) %all-to-all-start) | async-done | bytes 458784 | tf_op jit(solution)/shard_map/while/body/eval_jaxpr/all_to_all | solution.py:94
  644.0 7.9 convolution_convert_fusion.6
  676.6 5.9 all-to-all-done.2
  692.0 10.5 %all-to-all-done = bf16[8,4,7168]{2,1,0:T(4,128)(2,1)S(1)} async-done(((bf16[8,4,7168]{2,1,0:T(4,128)(2,1)}), bf16[8,4,7168]{2,1,0:T(4,128)(2,1)S(1)}, u32[]{:S(2)}, u32[]{:S(2)}) %all-to-all-start) | async-done | bytes 458784 | tf_op jit(solution)/shard_map/while/body/eval_jaxpr/all_to_all | solution.py:94
  707.0 7.9 convolution_convert_fusion.6
  739.6 5.9 all-to-all-done.2
  755.0 10.5 %all-to-all-done = bf16[8,4,7168]{2,1,0:T(4,128)(2,1)S(1)} async-done(((bf16[8,4,7168]{2,1,0:T(4,128)(2,1)}), bf16[8,4,7168]{2,1,0:T(4,128)(2,1)S(1)}, u32[]{:S(2)}, u32[]{:S(2)}) %all-to-all-start) | async-done | bytes 458784 | tf_op jit(solution)/shard_map/while/body/eval_jaxpr/all_to_all | solution.py:94
  770.0 7.9 convolution_convert_fusion.6
  802.5 5.9 all-to-all-done.2
  (251 shorter events, 270.4 us)
Async XLA Ops:
  7.2 355.6 %all-reduce.3.cloned.1.call-start = ((), (), s32[]{:S(2)}) async-start(), calls=%async_computation.3 | async-start | bytes 22020096 | tf_op jit(solution)/shard_map/psum | solution.py:12
  366.3 16.7 %all-to-all-start = ((bf16[8,4,7168]{2,1,0:T(4,128)(2,1)}), bf16[8,4,7168]{2,1,0:T(4,128)(2,1)S(1)}, u32[]{:S(2)}, u32[]{:S(2)}) async-start(bf16[8,4,7168]{2,1,0:T(4,128)(2,1)} %bitcast.92), calls=%async_computation | async-start | bytes 917504 | tf_op jit(solution)/shard_map/while/body/eval_jaxpr/all_to_all | solution.py:94
  396.4 16.9 %all-to-all-start.1 = ((bf16[8,4,7168]{2,1,0:T(4,128)(2,1)}), bf16[8,4,7168]{2,1,0:T(4,128)(2,1)S(1)}, u32[]{:S(2)}, u32[]{:S(2)}) async-start(bf16[8,4,7168]{2,1,0:T(4,128)(2,1)} %reshape.177), calls=%async_computation.1 | async-start | bytes 917504 | tf_op jit(solution)/shard_map/while/body/eval_jaxpr/all_to_all | solution.py:64
  414.5 14.1 %collective-permute-start = (bf16[8,7168]{1,0:T(8,128)(2,1)S(1)}, bf16[8,7168]{1,0:T(8,128)(2,1)S(1)}, u32[]{:S(2)}, u32[]{:S(2)}) collective-permute-start(bf16[8,7168]{1,0:T(8,128)(2,1)S(1)} %get-tuple-element.674), channel_id=1, source_target_pairs={{0,8},{8,16},{16,24},{1,9},{9,17},{17,25},{2,10},{10,18},{18,26},{... | collective-permute-start | bytes 344072 | tf_op jit(solution)/shard_map/while/body/eval_jaxpr/ppermute | solution.py:18
  416.6 10.7 %all-to-all-start.2 = ((bf16[8,1,4]{2,1,0:T(2,128)(2,1)}), bf16[8,1,4]{2,1,0:T(2,128)(2,1)S(1)}, u32[]{:S(2)}, u32[]{:S(2)}) async-start(bf16[8,1,4]{2,1,0:T(2,128)(2,1)} %copy.40), calls=%async_computation.2 | async-start | bytes 8192 | tf_op jit(solution)/shard_map/while/body/eval_jaxpr/all_to_all | solution.py:95
  432.0 17.1 %all-to-all-start = ((bf16[8,4,7168]{2,1,0:T(4,128)(2,1)}), bf16[8,4,7168]{2,1,0:T(4,128)(2,1)S(1)}, u32[]{:S(2)}, u32[]{:S(2)}) async-start(bf16[8,4,7168]{2,1,0:T(4,128)(2,1)} %bitcast.92), calls=%async_computation | async-start | bytes 917504 | tf_op jit(solution)/shard_map/while/body/eval_jaxpr/all_to_all | solution.py:94
  462.4 16.9 %all-to-all-start.1 = ((bf16[8,4,7168]{2,1,0:T(4,128)(2,1)}), bf16[8,4,7168]{2,1,0:T(4,128)(2,1)S(1)}, u32[]{:S(2)}, u32[]{:S(2)}) async-start(bf16[8,4,7168]{2,1,0:T(4,128)(2,1)} %reshape.177), calls=%async_computation.1 | async-start | bytes 917504 | tf_op jit(solution)/shard_map/while/body/eval_jaxpr/all_to_all | solution.py:64
  480.6 14.1 %collective-permute-start = (bf16[8,7168]{1,0:T(8,128)(2,1)S(1)}, bf16[8,7168]{1,0:T(8,128)(2,1)S(1)}, u32[]{:S(2)}, u32[]{:S(2)}) collective-permute-start(bf16[8,7168]{1,0:T(8,128)(2,1)S(1)} %get-tuple-element.674), channel_id=1, source_target_pairs={{0,8},{8,16},{16,24},{1,9},{9,17},{17,25},{2,10},{10,18},{18,26},{... | collective-permute-start | bytes 344072 | tf_op jit(solution)/shard_map/while/body/eval_jaxpr/ppermute | solution.py:18
  482.7 10.7 %all-to-all-start.2 = ((bf16[8,1,4]{2,1,0:T(2,128)(2,1)}), bf16[8,1,4]{2,1,0:T(2,128)(2,1)S(1)}, u32[]{:S(2)}, u32[]{:S(2)}) async-start(bf16[8,1,4]{2,1,0:T(2,128)(2,1)} %copy.40), calls=%async_computation.2 | async-start | bytes 8192 | tf_op jit(solution)/shard_map/while/body/eval_jaxpr/all_to_all | solution.py:95
  498.1 15.5 %all-to-all-start = ((bf16[8,4,7168]{2,1,0:T(4,128)(2,1)}), bf16[8,4,7168]{2,1,0:T(4,128)(2,1)S(1)}, u32[]{:S(2)}, u32[]{:S(2)}) async-start(bf16[8,4,7168]{2,1,0:T(4,128)(2,1)} %bitcast.92), calls=%async_computation | async-start | bytes 917504 | tf_op jit(solution)/shard_map/while/body/eval_jaxpr/all_to_all | solution.py:94
  526.9 16.2 %all-to-all-start.1 = ((bf16[8,4,7168]{2,1,0:T(4,128)(2,1)}), bf16[8,4,7168]{2,1,0:T(4,128)(2,1)S(1)}, u32[]{:S(2)}, u32[]{:S(2)}) async-start(bf16[8,4,7168]{2,1,0:T(4,128)(2,1)} %reshape.177), calls=%async_computation.1 | async-start | bytes 917504 | tf_op jit(solution)/shard_map/while/body/eval_jaxpr/all_to_all | solution.py:64
  544.4 13.4 %collective-permute-start = (bf16[8,7168]{1,0:T(8,128)(2,1)S(1)}, bf16[8,7168]{1,0:T(8,128)(2,1)S(1)}, u32[]{:S(2)}, u32[]{:S(2)}) collective-permute-start(bf16[8,7168]{1,0:T(8,128)(2,1)S(1)} %get-tuple-element.674), channel_id=1, source_target_pairs={{0,8},{8,16},{16,24},{1,9},{9,17},{17,25},{2,10},{10,18},{18,26},{... | collective-permute-start | bytes 344072 | tf_op jit(solution)/shard_map/while/body/eval_jaxpr/ppermute | solution.py:18
  561.2 15.3 %all-to-all-start = ((bf16[8,4,7168]{2,1,0:T(4,128)(2,1)}), bf16[8,4,7168]{2,1,0:T(4,128)(2,1)S(1)}, u32[]{:S(2)}, u32[]{:S(2)}) async-start(bf16[8,4,7168]{2,1,0:T(4,128)(2,1)} %bitcast.92), calls=%async_computation | async-start | bytes 917504 | tf_op jit(solution)/shard_map/while/body/eval_jaxpr/all_to_all | solution.py:94
  589.9 16.2 %all-to-all-start.1 = ((bf16[8,4,7168]{2,1,0:T(4,128)(2,1)}), bf16[8,4,7168]{2,1,0:T(4,128)(2,1)S(1)}, u32[]{:S(2)}, u32[]{:S(2)}) async-start(bf16[8,4,7168]{2,1,0:T(4,128)(2,1)} %reshape.177), calls=%async_computation.1 | async-start | bytes 917504 | tf_op jit(solution)/shard_map/while/body/eval_jaxpr/all_to_all | solution.py:64
  607.3 13.4 %collective-permute-start = (bf16[8,7168]{1,0:T(8,128)(2,1)S(1)}, bf16[8,7168]{1,0:T(8,128)(2,1)S(1)}, u32[]{:S(2)}, u32[]{:S(2)}) collective-permute-start(bf16[8,7168]{1,0:T(8,128)(2,1)S(1)} %get-tuple-element.674), channel_id=1, source_target_pairs={{0,8},{8,16},{16,24},{1,9},{9,17},{17,25},{2,10},{10,18},{18,26},{... | collective-permute-start | bytes 344072 | tf_op jit(solution)/shard_map/while/body/eval_jaxpr/ppermute | solution.py:18
  624.2 15.3 %all-to-all-start = ((bf16[8,4,7168]{2,1,0:T(4,128)(2,1)}), bf16[8,4,7168]{2,1,0:T(4,128)(2,1)S(1)}, u32[]{:S(2)}, u32[]{:S(2)}) async-start(bf16[8,4,7168]{2,1,0:T(4,128)(2,1)} %bitcast.92), calls=%async_computation | async-start | bytes 917504 | tf_op jit(solution)/shard_map/while/body/eval_jaxpr/all_to_all | solution.py:94
  652.9 16.2 %all-to-all-start.1 = ((bf16[8,4,7168]{2,1,0:T(4,128)(2,1)}), bf16[8,4,7168]{2,1,0:T(4,128)(2,1)S(1)}, u32[]{:S(2)}, u32[]{:S(2)}) async-start(bf16[8,4,7168]{2,1,0:T(4,128)(2,1)} %reshape.177), calls=%async_computation.1 | async-start | bytes 917504 | tf_op jit(solution)/shard_map/while/body/eval_jaxpr/all_to_all | solution.py:64
  670.3 13.4 %collective-permute-start = (bf16[8,7168]{1,0:T(8,128)(2,1)S(1)}, bf16[8,7168]{1,0:T(8,128)(2,1)S(1)}, u32[]{:S(2)}, u32[]{:S(2)}) collective-permute-start(bf16[8,7168]{1,0:T(8,128)(2,1)S(1)} %get-tuple-element.674), channel_id=1, source_target_pairs={{0,8},{8,16},{16,24},{1,9},{9,17},{17,25},{2,10},{10,18},{18,26},{... | collective-permute-start | bytes 344072 | tf_op jit(solution)/shard_map/while/body/eval_jaxpr/ppermute | solution.py:18
  687.2 15.3 %all-to-all-start = ((bf16[8,4,7168]{2,1,0:T(4,128)(2,1)}), bf16[8,4,7168]{2,1,0:T(4,128)(2,1)S(1)}, u32[]{:S(2)}, u32[]{:S(2)}) async-start(bf16[8,4,7168]{2,1,0:T(4,128)(2,1)} %bitcast.92), calls=%async_computation | async-start | bytes 917504 | tf_op jit(solution)/shard_map/while/body/eval_jaxpr/all_to_all | solution.py:94
  715.8 16.2 %all-to-all-start.1 = ((bf16[8,4,7168]{2,1,0:T(4,128)(2,1)}), bf16[8,4,7168]{2,1,0:T(4,128)(2,1)S(1)}, u32[]{:S(2)}, u32[]{:S(2)}) async-start(bf16[8,4,7168]{2,1,0:T(4,128)(2,1)} %reshape.177), calls=%async_computation.1 | async-start | bytes 917504 | tf_op jit(solution)/shard_map/while/body/eval_jaxpr/all_to_all | solution.py:64
  733.3 13.4 %collective-permute-start = (bf16[8,7168]{1,0:T(8,128)(2,1)S(1)}, bf16[8,7168]{1,0:T(8,128)(2,1)S(1)}, u32[]{:S(2)}, u32[]{:S(2)}) collective-permute-start(bf16[8,7168]{1,0:T(8,128)(2,1)S(1)} %get-tuple-element.674), channel_id=1, source_target_pairs={{0,8},{8,16},{16,24},{1,9},{9,17},{17,25},{2,10},{10,18},{18,26},{... | collective-permute-start | bytes 344072 | tf_op jit(solution)/shard_map/while/body/eval_jaxpr/ppermute | solution.py:18
  750.1 15.3 %all-to-all-start = ((bf16[8,4,7168]{2,1,0:T(4,128)(2,1)}), bf16[8,4,7168]{2,1,0:T(4,128)(2,1)S(1)}, u32[]{:S(2)}, u32[]{:S(2)}) async-start(bf16[8,4,7168]{2,1,0:T(4,128)(2,1)} %bitcast.92), calls=%async_computation | async-start | bytes 917504 | tf_op jit(solution)/shard_map/while/body/eval_jaxpr/all_to_all | solution.py:94
  778.8 16.2 %all-to-all-start.1 = ((bf16[8,4,7168]{2,1,0:T(4,128)(2,1)}), bf16[8,4,7168]{2,1,0:T(4,128)(2,1)S(1)}, u32[]{:S(2)}, u32[]{:S(2)}) async-start(bf16[8,4,7168]{2,1,0:T(4,128)(2,1)} %reshape.177), calls=%async_computation.1 | async-start | bytes 917504 | tf_op jit(solution)/shard_map/while/body/eval_jaxpr/all_to_all | solution.py:64
  796.2 13.4 %collective-permute-start = (bf16[8,7168]{1,0:T(8,128)(2,1)S(1)}, bf16[8,7168]{1,0:T(8,128)(2,1)S(1)}, u32[]{:S(2)}, u32[]{:S(2)}) collective-permute-start(bf16[8,7168]{1,0:T(8,128)(2,1)S(1)} %get-tuple-element.674), channel_id=1, source_target_pairs={{0,8},{8,16},{16,24},{1,9},{9,17},{17,25},{2,10},{10,18},{18,26},{... | collective-permute-start | bytes 344072 | tf_op jit(solution)/shard_map/while/body/eval_jaxpr/ppermute | solution.py:18
  (9 other events, 743.2 us)
Sparse Core Ops, SparseCore 0:
  19.3 343.4 all-reduce.2
where the time goes:
time: 821 us; the launch traced here: 818 us
  waiting for transfers between devices  495 us (60%)
  matrix products  152 us (19%)
  starting transfers between devices  85.9 us (10%)
  other arithmetic  35.9 us (4%)
  local copies, waits for them, and re-layouts  24.2 us (3%)
  between operations  15.9 us (2%)
  loops' own time  9.38 us (1%)
    psum x1, waiting for transfers between devices, spread(): return lax.psum(block, axis)  344 us
    all_to_all x7, waiting for transfers between devices, apply_layer(): lax.all_to_all(send_rows, 'ep', split_axis=0, concat_axis=0, tiled=True)  76.5 us
    dot_general x7, matrix products, expert_rows(): jnp.dot(home_act, down_w, preferred_element_type=jnp.float32)  55.2 us
    all_to_all x7, waiting for transfers between devices, apply_layer(): lax.all_to_all(send_flags, 'ep', split_axis=0, concat_axis=0, tiled=True)  41 us
    dot_general x7, matrix products, apply_layer(): jnp.dot(local_act, copy_down, preferred_element_type=jnp.float32)  36.9 us
    all_to_all x7, waiting for transfers between devices, work_both(): lax.all_to_all(home_part, 'ep', split_axis=0, concat_axis=0, tiled=True)  33.6 us
    dot_general x7, matrix products, expert_rows(): gate_value = jnp.dot(flat_rows, gate_w, preferred_element_type=jnp.float32)  31 us
    all_to_all x7, starting transfers between devices, apply_layer(): lax.all_to_all(send_flags, 'ep', split_axis=0, concat_axis=0, tiled=True)  26.7 us
  transfers between devices with their start and end apart: 29, of which 22 were waited for; matrix products, arithmetic and copies ran while one was open for 9% of the time, Pallas kernels for 0%

commit v1 on v0

--- a/solution.py
+++ b/solution.py
@@ -9,7 +9,7 @@
 
 def spread(block, axis, source):
     block = jnp.where(lax.axis_index(axis) == source, block, jnp.zeros_like(block))
-    return lax.psum(block, axis)
+    return jnp.sum(lax.all_gather(block, axis), axis=0)
 
 
 def shifted(block, axis, distance):

time: 821 us -> 2170 us (2.64)
  waiting for transfers between devices: 495 us -> 1800 us
  other arithmetic: 35.9 us -> 78.7 us
    all_gather x0 -> x3, waiting for transfers between devices: none -> 1650 us  [spread(): return jnp.sum(lax.all_gather(block, axis), axis=0)]
    psum x1 -> x0, waiting for transfers between devices: 344 us -> none  [spread(): return lax.psum(block, axis)]
    reduce_sum x0 -> x3, other arithmetic: none -> 39.5 us  [spread(): return jnp.sum(lax.all_gather(block, axis), axis=0)]
  transfers between devices with their start and end apart: 29 -> 31, of which waited for: 22 -> 24; matrix products, arithmetic and copies ran while one was open for 9% -> 5% of each run, Pallas kernels for 0% -> 0%
where the time goes in v1:
time: 2170 us; the launch traced here: 2160 us
  waiting for transfers between devices  1800 us (83%)
  matrix products  153 us (7%)
  starting transfers between devices  86.9 us (4%)
  other arithmetic  78.7 us (4%)
  local copies, waits for them, and re-layouts  24.2 us (1%)
    all_gather x3, waiting for transfers between devices, spread(): return jnp.sum(lax.all_gather(block, axis), axis=0)  1650 us
    all_to_all x7, waiting for transfers between devices, apply_layer(): lax.all_to_all(send_rows, 'ep', split_axis=0, concat_axis=0, tiled=True)  75.8 us
    dot_general x7, matrix products, expert_rows(): jnp.dot(home_act, down_w, preferred_element_type=jnp.float32)  55.2 us
  transfers between devices with their start and end apart: 31, of which 24 were waited for; matrix products, arithmetic and copies ran while one was open for 5% of the time, Pallas kernels for 0%

profile of v1, /device:TPU:0, one launch (start us, length us, event | category | flops | bytes accessed | tf_op | source)
XLA Modules:
  0.0 2164.9 jit_solution(12279119802482122645)
XLA Ops:
  21.8 552.5 %all-gather.4.cloned.1.call-done = bf16[8,7168,256]{2,1,0:T(8,128)(2,1)} async-done(((bf16[1,7168,256]{2,1,0:T(8,128)(2,1)}), bf16[8,7168,256]{2,1,0:T(8,128)(2,1)}) %all-gather.4.cloned.1.call-update) | async-done | bytes 29360144 | tf_op jit(solution)/shard_map/all_gather | solution.py:12
  574.3 13.3 reduce_sum.167
  587.6 547.2 %all-gather.6.cloned.1.call-done = bf16[8,7168,256]{2,1,0:T(8,128)(2,1)} async-done(((bf16[1,7168,256]{2,1,0:T(8,128)(2,1)}), bf16[8,7168,256]{2,1,0:T(8,128)(2,1)}) %all-gather.6.cloned.1.call-update) | async-done | bytes 29360144 | tf_op jit(solution)/shard_map/all_gather | solution.py:12
  1134.8 13.3 reduce_sum.168
  1148.2 547.2 %all-gather.8.cloned.1.call-done = bf16[8,256,7168]{2,1,0:T(8,128)(2,1)} async-done(((bf16[1,256,7168]{2,1,0:T(8,128)(2,1)}), bf16[8,256,7168]{2,1,0:T(8,128)(2,1)}) %all-gather.8.cloned.1.call-update) | async-done | bytes 29360144 | tf_op jit(solution)/shard_map/all_gather | solution.py:12
  1695.4 12.8 reduce_sum.169
  1708.3 448.1 %while.22 = (s32[]{:T(128)}, bf16[8,7168]{1,0:T(8,128)(2,1)S(1)}, bf16[4,8,7168]{2,1,0:T(8,128)(2,1)S(1)}, f32[]{:T(128)}, f32[]{:T(128)}, /*index=5*/pred[]{:T(...) while((s32[]{:T(128)}, bf16[8,7168]{1,0:T(8,128)(2,1)S(1)}, ...), condition=%wide.region_14.15_spmd.clone.clone, body=%wide.region_3.14_spmd.clone.clone.sunk | while | flops 808455232 | bytes 45640856 | solution.py:138
  1717.8 11.8 all-to-all-done
  1734.2 7.9 convolution_convert_fusion.6
  1768.2 5.7 all-to-all-done.2
  1783.6 12.1 all-to-all-done
  1800.3 7.9 convolution_convert_fusion.6
  1834.3 5.7 all-to-all-done.2
  1849.7 10.6 all-to-all-done
  1864.8 7.9 convolution_convert_fusion.6
  1912.9 10.3 all-to-all-done
  1927.8 7.9 convolution_convert_fusion.6
  1975.9 10.3 all-to-all-done
  1990.8 7.9 convolution_convert_fusion.6
  2023.5 5.7 all-to-all-done.2
  2038.9 10.3 all-to-all-done
  2053.8 7.9 convolution_convert_fusion.6
  2101.9 10.3 all-to-all-done
  2116.8 7.9 convolution_convert_fusion.6
  (259 shorter events, 304.3 us)
Async XLA Ops:
  7.2 567.1 %all-gather.4.cloned.1.call-start = ((), (), s32[]{:S(2)}) async-start(), calls=%async_computation.3 | async-start | bytes 33030144 | tf_op jit(solution)/shard_map/all_gather | solution.py:12
  12.4 1122.4 %all-gather.6.cloned.1.call-start = ((), (), s32[]{:S(2)}) async-start(), calls=%async_computation.4 | async-start | bytes 33030144 | tf_op jit(solution)/shard_map/all_gather | solution.py:12
  17.1 1678.3 %all-gather.8.cloned.1.call-start = ((), (), s32[]{:S(2)}) async-start(), calls=%async_computation.5 | async-start | bytes 33030144 | tf_op jit(solution)/shard_map/all_gather | solution.py:12
  1711.8 17.8 all-to-all-start
  1743.0 16.9 all-to-all-start.1
  1761.1 14.1 collective-permute-start
  1778.6 17.1 all-to-all-start
  1809.1 16.9 all-to-all-start.1
  1827.2 14.1 collective-permute-start
  1844.7 15.5 all-to-all-start
  1873.6 16.2 all-to-all-start.1
  1891.1 13.4 collective-permute-start
  1907.9 15.3 all-to-all-start
  1936.6 16.2 all-to-all-start.1
  1954.0 13.4 collective-permute-start
  1970.9 15.3 all-to-all-start
  1999.6 16.2 all-to-all-start.1
  2017.0 13.4 collective-permute-start
  2033.9 15.3 all-to-all-start
  2062.6 16.2 all-to-all-start.1
  2080.0 13.4 collective-permute-start
  2096.9 15.3 all-to-all-start
  2125.6 16.2 all-to-all-start.1
  2143.0 13.4 collective-permute-start
  (10 other events, 1192.7 us)
Sparse Core Ops, SparseCore 0:
  12.5 561.7 all-gather.3
  575.8 558.9 all-gather.5
  1136.4 558.9 all-gather.7
